TPU v7x, 32 devices: a whole 2x2x4 slice. The times are simulated.
32 devices in a mesh: groups: 2 (over y), tok: 16 (over z, x, core).
Axes of the slice: x: 2, y: 2, z: 4, core: 2. Of those that a mesh axis runs over, the one named last changes fastest.
Arguments:
- queries: bfloat16 [2048, 2048], P(('groups', 'tok')), parts along dimension 0, may hold values from -256 to 256, as said below
- fresh_keys: bfloat16 [2048, 2048], P(('groups', 'tok')), parts along dimension 0, may hold values from -6 to 6, as said below
- fresh_values: bfloat16 [2048, 2048], P(('groups', 'tok')), parts along dimension 0, may hold values from -6 to 6
- stale_keys: bfloat16 [2048, 2048], P(('groups', 'tok')), parts along dimension 0, may hold values from -6 to 6
- stale_values: bfloat16 [2048, 2048], P(('groups', 'tok')), parts along dimension 0, may hold values from -6 to 6
- patch_starts: int32 [32], P('groups'), parts along dimension 0, may hold values from 0 to 1023, as said below
- order_starts: int32 [32], P('groups'), parts along dimension 0, may hold values from 0 to 1023, as said below
Outputs:
- attended: bfloat16 [2048, 2048], P(('groups', 'tok')), parts along dimension 0
There are 2 independent parts, one for each index of `groups`. A program takes and returns all parts, laid end to end along the dimension named above; each array names one. Nothing has to cross between parts.
Inputs may be any that keep to these rules, and one draw needn't show every extreme that they name: `patch_starts`: strictly increasing; the first entry is 0. `order_starts`: the entries of patch_starts, each once, in processing order. `queries`: entries are finite. `fresh_keys`: entries are finite.
All inputs are finite; a program needn't handle non-finite values.
Results may differ from a plain program's by a relative error of at most 0.0049.
Values may be sent and summed in bfloat16 or wider, within the bound.
A program may use at most 128 MiB of HBM per device.

v0:
```python
import math

import jax
import jax.numpy as jnp
from jax import lax
from jax.sharding import PartitionSpec as P

HEADS = 16
HEAD_DIM = 128


def token_ranks(positions, patch_starts, order_starts):
    patch_count = patch_starts.shape[0]
    slot_ids = jnp.arange(patch_count, dtype=jnp.int32)
    patch_of = jnp.sum((patch_starts[None, :] <= positions[:, None]).astype(jnp.int32), axis=1) - 1
    matches = (order_starts[:, None] == patch_starts[None, :]).astype(jnp.int32)
    rank_of = jnp.sum(matches * slot_ids[:, None], axis=0)
    one_hot = (patch_of[:, None] == slot_ids[None, :]).astype(jnp.int32)
    return jnp.sum(one_hot * rank_of[None, :], axis=1)


def masked_scores(query_block, query_rank, key_stack, key_rank):
    dims = (((1,), (1,)), ((), ()))
    score_scale = 1.0 / math.sqrt(query_block.shape[-1])
    fresh_scores = (
        lax.dot_general(query_block, key_stack[0], dims, preferred_element_type=jnp.float32)
        * score_scale
    )
    stale_scores = (
        lax.dot_general(query_block, key_stack[2], dims, preferred_element_type=jnp.float32)
        * score_scale
    )
    fresh_ok = key_rank[None, :] <= query_rank[:, None]
    fresh_scores = jnp.where(fresh_ok, fresh_scores, -jnp.inf)
    stale_scores = jnp.where(fresh_ok, -jnp.inf, stale_scores)
    return (fresh_scores, stale_scores)


def attend_block(query_block, query_rank, key_stack, key_rank):
    fresh_scores, stale_scores = masked_scores(query_block, query_rank, key_stack, key_rank)
    row_max = jnp.maximum(jnp.max(fresh_scores, axis=1), jnp.max(stale_scores, axis=1))[:, None]
    fresh_exp = jnp.exp(fresh_scores - row_max)
    stale_exp = jnp.exp(stale_scores - row_max)
    row_total = jnp.sum(fresh_exp, axis=1, keepdims=True) + jnp.sum(
        stale_exp, axis=1, keepdims=True
    )
    fresh_probs = (fresh_exp / row_total).astype(jnp.bfloat16)
    stale_probs = (stale_exp / row_total).astype(jnp.bfloat16)
    mixed = jnp.dot(fresh_probs, key_stack[1], preferred_element_type=jnp.float32)
    mixed = mixed + jnp.dot(stale_probs, key_stack[3], preferred_element_type=jnp.float32)
    return mixed.astype(jnp.bfloat16)


def attend_rows(query_rows, query_rank, key_stack, key_rank):
    row_count = query_rows.shape[0]
    block_rows = 512
    blocks = row_count // block_rows

    def one_block(inputs):
        return attend_block(inputs[0], inputs[1], key_stack, key_rank)

    result = lax.map(
        one_block,
        (
            query_rows.reshape(blocks, block_rows, query_rows.shape[1]),
            query_rank.reshape(blocks, block_rows),
        ),
    )
    return result.reshape(row_count, query_rows.shape[1])


def shards(queries, fresh_keys, fresh_values, stale_keys, stale_values, patch_starts, order_starts):
    devices = lax.axis_size("tok")
    tok_dev, row_width = queries.shape
    group_size = devices // HEADS
    slab_rows = tok_dev // group_size
    my_index = lax.axis_index("tok")
    member = my_index % group_size
    query_slabs = (
        queries.reshape(group_size, slab_rows, HEADS, HEAD_DIM)
        .transpose(2, 0, 1, 3)
        .reshape(devices, slab_rows, HEAD_DIM)
    )
    query_rows = lax.all_to_all(query_slabs, "tok", split_axis=0, concat_axis=0, tiled=True)
    stacked = jnp.stack([fresh_keys, fresh_values, stale_keys, stale_values]).reshape(
        4, tok_dev, HEADS, HEAD_DIM
    )
    sender_base = jnp.arange(devices, dtype=jnp.int32)[:, None] * tok_dev
    slab_offsets = jnp.arange(slab_rows, dtype=jnp.int32)[None, :]
    query_pos = (sender_base + member * slab_rows + slab_offsets).reshape(-1)
    by_head = stacked.transpose(0, 2, 1, 3)[:, :, None]
    spread = jnp.broadcast_to(by_head, (4, HEADS, group_size, tok_dev, HEAD_DIM)).reshape(
        4, devices, tok_dev, HEAD_DIM
    )
    arrived = lax.all_to_all(spread, "tok", split_axis=1, concat_axis=1, tiled=True)
    key_stack = arrived.reshape(4, devices * tok_dev, HEAD_DIM)
    key_rank = token_ranks(
        jnp.arange(devices * tok_dev, dtype=jnp.int32), patch_starts, order_starts
    )
    query_rank = token_ranks(query_pos, patch_starts, order_starts)
    attended = attend_rows(
        query_rows.reshape(devices * slab_rows, HEAD_DIM), query_rank, key_stack, key_rank
    )
    returned = lax.all_to_all(
        attended.reshape(devices, slab_rows, HEAD_DIM),
        "tok",
        split_axis=0,
        concat_axis=0,
        tiled=True,
    )
    return (
        returned.reshape(HEADS, group_size, slab_rows, HEAD_DIM)
        .transpose(1, 2, 0, 3)
        .reshape(tok_dev, row_width)
    )


def solution(mesh):
    placed = (
        P(("groups", "tok"), None),
        P(("groups", "tok"), None),
        P(("groups", "tok"), None),
        P(("groups", "tok"), None),
        P(("groups", "tok"), None),
        P("groups"),
        P("groups"),
    )
    return jax.shard_map(
        shards, mesh=mesh, in_specs=placed, out_specs=P(("groups", "tok"), None), check_vma=False
    )
```

profile of v0, /device:TPU:0, one launch (start us, length us, event | category | flops | bytes accessed | tf_op | source)
XLA Modules:
  0.0 72.3 jit_solution(15579702160136215881)
XLA Ops:
  0.0 1.0 %copy.24 = bf16[8,8,16,128]{3,2,1,0:T(8,128)(2,1)S(1)} copy(bf16[8,8,16,128]{3,1,2,0:T(8,128)(2,1)} %bitcast.87) | data formatting | bytes 524288
  1.0 1.0 %copy.25 = bf16[8,8,16,128]{3,2,1,0:T(8,128)(2,1)S(1)} copy(bf16[8,8,16,128]{3,1,2,0:T(8,128)(2,1)} %bitcast.88) | data formatting | bytes 524288
  2.0 1.0 %copy.26 = bf16[8,8,16,128]{3,2,1,0:T(8,128)(2,1)S(1)} copy(bf16[8,8,16,128]{3,1,2,0:T(8,128)(2,1)} %bitcast.89) | data formatting | bytes 524288
  3.0 1.0 %copy.27 = bf16[8,8,16,128]{3,2,1,0:T(8,128)(2,1)S(1)} copy(bf16[8,8,16,128]{3,1,2,0:T(8,128)(2,1)} %bitcast.90) | data formatting | bytes 524288
  4.0 0.1 maximum_bitcast_fusion
  4.1 0.0 copy-start
  4.1 1.3 %copy.20 = bf16[4,16,64,128]{3,2,0,1:T(8,128)(2,1)} copy(bf16[4,16,64,128]{3,1,2,0:T(8,128)(2,1)S(1)} %maximum_bitcast_fusion) | data formatting | bytes 2097152 | tf_op jit(solution)/shard_map/transpose | solution.py:91
  5.4 0.0 copy-start.1
  5.4 0.0 copy-start.2
  5.4 7.5 %all-to-all-start.1 = ((bf16[4,16,64,128]{3,2,0,1:T(8,128)(2,1)}), bf16[4,16,64,128]{3,2,0,1:T(8,128)(2,1)S(1)}, u32[]{:S(2)}, u32[]{:S(2)}) async-start(bf16[4,16,64,128]{3,2,0,1:T(8,128)(2,1)} %copy.20), calls=%async_computation.1 | async-start | bytes 2097152 | tf_op jit(solution)/shard_map/all_to_all | solution.py:95
  12.9 0.0 copy-done
  13.0 0.8 %copy.32 = bf16[1,64,16,128]{3,1,2,0:T(8,128)(2,1)} copy(bf16[1,64,16,128]{3,2,1,0:T(8,128)(2,1)S(1)} %bitcast.82) | data formatting | bytes 524288 | tf_op jit(solution)/shard_map/reshape | solution.py:80
  13.8 0.1 iota_add_fusion
  13.8 22.0 %all-to-all-done.1 = bf16[4,16,64,128]{3,2,0,1:T(8,128)(2,1)S(1)} async-done(((bf16[4,16,64,128]{3,2,0,1:T(8,128)(2,1)}), bf16[4,16,64,128]{3,2,0,1:T(8,128)(2,1)S(1)}, u32[]{:S(2)}, u32[]{:S(2)}) %all-to-all-start.1) | async-done | bytes 1048608 | tf_op jit(solution)/shard_map/all_to_all | solution.py:95
  35.8 6.8 %all-to-all-start = ((bf16[16,64,128]{2,1,0:T(8,128)(2,1)}), bf16[16,64,128]{2,1,0:T(8,128)(2,1)S(1)}, u32[]{:S(2)}, u32[]{:S(2)}) async-start(bf16[16,64,128]{2,1,0:T(8,128)(2,1)} %bitcast.62), calls=%async_computation | async-start | bytes 524288 | tf_op jit(solution)/shard_map/all_to_all | solution.py:84
  42.6 0.0 copy-done.1
  42.6 0.0 copy-done.2
  42.6 0.1 select_reduce_fusion.2
  42.7 0.1 add.53
  42.8 0.1 convert_reduce_fusion
  42.9 0.1 select_reduce_fusion
  43.0 0.1 copy.21
  43.1 9.5 %all-to-all-done = bf16[16,64,128]{2,1,0:T(8,128)(2,1)S(1)} async-done(((bf16[16,64,128]{2,1,0:T(8,128)(2,1)}), bf16[16,64,128]{2,1,0:T(8,128)(2,1)S(1)}, u32[]{:S(2)}, u32[]{:S(2)}) %all-to-all-start) | async-done | bytes 262176 | tf_op jit(solution)/shard_map/all_to_all | solution.py:84
  52.6 6.0 %while.10 = (s32[]{:T(128)}, bf16[2,512,128]{2,1,0:T(8,128)(2,1)S(1)}, s32[1024]{0:T(1024)S(1)}, s32[2,512]{1,0:T(2,128)S(1)}, bf16[2,512,128]{2,1,0:T(8,128)(2,...) while((s32[]{:T(128)}, bf16[2,512,128]{2,1,0:T(8,128)(2,1)S(1)}, s32[1024]{0:T(1024)S(1)}, ...), condition=%wide.region_10.11_spmd, body=%wide.region_5.10_spmd.sunk | while | flops 546438144 | bytes 14596189 | solution.py:62
  52.6 0.5 fusion.31
  53.2 0.5 fusion.32
  53.7 0.7 fusion.33
  54.4 0.6 fusion.34
  55.0 0.6 fusion.35
  55.7 0.5 fusion.31
  56.2 0.5 fusion.32
  56.7 0.7 fusion.33
  57.5 0.6 fusion.34
  58.0 0.6 fusion.35
  58.7 12.7 %all_to_all.15 = bf16[16,64,128]{2,1,0:T(8,128)(2,1)S(1)} all-to-all(bf16[16,64,128]{2,1,0:T(8,128)(2,1)S(1)} %bitcast.93), channel_id=1, replica_groups=mesh['groups'=2,'tok'=16] {'tok'}, dimensions={0} | all-to-all | bytes 524288 | tf_op jit(solution)/shard_map/all_to_all | solution.py:104
  71.3 0.2 copy.22
  71.5 0.8 %copy.31 = bf16[8,8,16,128]{3,1,2,0:T(8,128)(2,1)} copy(bf16[8,8,16,128]{3,2,1,0:T(8,128)(2,1)S(1)} %bitcast.81) | data formatting | bytes 524288
  (11 shorter events, 0.1 us)
Async XLA Ops:
  4.1 8.8 %copy-start = (bf16[64,2048]{1,0:T(8,128)(2,1)S(1)}, bf16[64,2048]{1,0:T(8,128)(2,1)}, u32[]{:S(2)}) copy-start(bf16[64,2048]{1,0:T(8,128)(2,1)} %param.9) | copy-start | bytes 786436
  5.4 37.2 %copy-start.1 = (s32[16]{0:T(128)S(1)}, s32[16]{0:T(128)}, u32[]{:S(2)}) copy-start(s32[16]{0:T(128)} %param.14) | copy-start | bytes 196
  5.4 37.2 %copy-start.2 = (s32[16]{0:T(128)S(1)}, s32[16]{0:T(128)}, u32[]{:S(2)}) copy-start(s32[16]{0:T(128)} %param.15) | copy-start | bytes 196
  5.4 30.4 %all-to-all-start.1 = ((bf16[4,16,64,128]{3,2,0,1:T(8,128)(2,1)}), bf16[4,16,64,128]{3,2,0,1:T(8,128)(2,1)S(1)}, u32[]{:S(2)}, u32[]{:S(2)}) async-start(bf16[4,16,64,128]{3,2,0,1:T(8,128)(2,1)} %copy.20), calls=%async_computation.1 | async-start | bytes 2097152 | tf_op jit(solution)/shard_map/all_to_all | solution.py:95
  35.8 16.8 %all-to-all-start = ((bf16[16,64,128]{2,1,0:T(8,128)(2,1)}), bf16[16,64,128]{2,1,0:T(8,128)(2,1)S(1)}, u32[]{:S(2)}, u32[]{:S(2)}) async-start(bf16[16,64,128]{2,1,0:T(8,128)(2,1)} %bitcast.62), calls=%async_computation | async-start | bytes 524288 | tf_op jit(solution)/shard_map/all_to_all | solution.py:84
where the time goes:
time: 72.7 us; the launch traced here: 72.3 us
  waiting for transfers between devices  31.5 us (43%)
  starting transfers between devices  14.3 us (20%)
  blocking collectives  12.7 us (17%)
  local copies, waits for them, and re-layouts  7.16 us (10%)
  matrix products  4.5 us (6%)
  other arithmetic  1.96 us (3%)
    all_to_all x1, waiting for transfers between devices, shards(): lax.all_to_all(spread, 'tok', split_axis=1, concat_axis=1, tiled=True)  22 us
    all_to_all x1, blocking collectives, shards(): lax.all_to_all(attended.reshape(devices, slab_rows, HEAD_DIM), 'tok', spl...  12.7 us
    all_to_all x1, waiting for transfers between devices, shards(): lax.all_to_all(query_slabs, 'tok', split_axis=0, concat_axis=0, tiled=True)  9.51 us
    all_to_all x1, starting transfers between devices, shards(): lax.all_to_all(spread, 'tok', split_axis=1, concat_axis=1, tiled=True)  7.52 us
    all_to_all x1, starting transfers between devices, shards(): lax.all_to_all(query_slabs, 'tok', split_axis=0, concat_axis=0, tiled=True)  6.79 us
    unnamed x12, local copies, waits for them, and re-layouts  4.77 us
  transfers between devices with their start and end apart: 2, of which 2 were waited for; matrix products, arithmetic and copies ran while one was open for 2% of the time, Pallas kernels for 0%

commit v1 on v0

v1 whole, which is shorter than its diff:
```python
import functools
import math

import jax
import jax.numpy as jnp
from jax import lax
from jax.experimental import pallas as pl
from jax.experimental.pallas import tpu as pltpu
from jax.sharding import PartitionSpec as P

HEADS = 16
HEAD_DIM = 128
MESH = pl.DeviceIdType.MESH


def attention_kernel(
    devices,
    patch_starts,
    order_starts,
    queries,
    fresh_keys,
    stale_keys,
    fresh_values,
    stale_values,
    out_ref,
    q_buf,
    kv_buf,
    p_fresh,
    p_stale,
    o_buf,
    q_rank,
    k_rank,
    send_sems,
    recv_sems,
    own_sem,
    out_send,
    out_recv,
):
    me = lax.axis_index("tok")
    tok_dev = queries.shape[0]
    group_size = devices // HEADS
    slab = tok_dev // group_size
    tokens = devices * tok_dev
    rows = devices * slab
    my_head = me // group_size
    my_member = me % group_size
    barrier = pltpu.get_barrier_semaphore()

    def peer_of(step):
        return lax.rem(me + step, devices)

    def columns(head):
        return pl.ds(pl.multiple_of(head * HEAD_DIM, HEAD_DIM), HEAD_DIM)

    def row_slab(index, size):
        return pl.ds(pl.multiple_of(index * size, size), size)

    def greet(step, carry):
        pl.semaphore_signal(barrier, inc=1, device_id={"tok": peer_of(step)}, device_id_type=MESH)
        return carry

    lax.fori_loop(1, devices, greet, 0)

    sources = (queries, fresh_keys, stale_keys, fresh_values, stale_values)

    def source_view(which, device):
        head, member = device // group_size, device % group_size
        if which == 0:
            return queries.at[row_slab(member, slab), columns(head)]
        return sources[which].at[:, columns(head)]

    def landing(which, device):
        if which == 0:
            return q_buf.at[row_slab(device, slab), :]
        return kv_buf.at[which - 1, row_slab(device, tok_dev), :]

    own = [
        pltpu.make_async_copy(source_view(which, me), landing(which, me), own_sem.at[which])
        for which in range(5)
    ]
    for copy in own:
        copy.start()
    pl.semaphore_wait(barrier, devices - 1)

    for which in range(5):

        def send(step, carry, which=which):
            peer = peer_of(step)
            pltpu.make_async_remote_copy(
                src_ref=source_view(which, peer),
                dst_ref=landing(which, me),
                send_sem=send_sems.at[which],
                recv_sem=recv_sems.at[which],
                device_id={"tok": peer},
                device_id_type=MESH,
            ).start()
            return carry

        lax.fori_loop(1, devices, send, 0)

    patches = patch_starts.shape[0]
    starts = [patch_starts[p] for p in range(patches)]
    orders = [order_starts[p] for p in range(patches)]
    ranks = []
    for p in range(patches):
        rank = jnp.int32(0)
        for i in range(patches):
            rank = rank + jnp.where(orders[i] == starts[p], jnp.int32(i), jnp.int32(0))
        ranks.append(rank)
    jumps = [ranks[0]] + [ranks[p] - ranks[p - 1] for p in range(1, patches)]

    def rank_at(positions):
        total = jnp.zeros(positions.shape, jnp.int32)
        for p in range(patches):
            total = total + jnp.where(positions >= starts[p], jumps[p], 0)
        return total

    k_rank[...] = rank_at(lax.broadcasted_iota(jnp.int32, k_rank.shape, 1))

    def fill_rank(device, carry):
        base = device * tok_dev + my_member * slab
        q_rank[row_slab(device, slab), :] = rank_at(
            base + lax.broadcasted_iota(jnp.int32, (slab, HEAD_DIM), 0)
        )
        return carry

    lax.fori_loop(0, devices, fill_rank, 0)

    def all_of(which):
        size = (devices - 1) * (slab if which == 0 else tok_dev)
        return q_buf.at[0:size, :] if which == 0 else kv_buf.at[which - 1, 0:size, :]

    def arrived(which):
        view = all_of(which)
        pltpu.make_async_copy(view, view, recv_sems.at[which]).wait()
        own[which].wait()

    for which in range(3):
        arrived(which)

    score_scale = 1.0 / math.sqrt(HEAD_DIM)
    block = max(slab, min(rows, (1 << 18) // tokens))
    blocks = rows // block
    dims = (((1,), (1,)), ((), ()))

    def probs_block(i, carry):
        at = row_slab(i, block)
        q = q_buf[at, :]
        fresh = lax.dot_general(q, kv_buf[0], dims, preferred_element_type=jnp.float32)
        stale = lax.dot_general(q, kv_buf[1], dims, preferred_element_type=jnp.float32)
        fresh_ok = k_rank[0:1, :] <= q_rank[at, 0:1]
        scores = jnp.where(fresh_ok, fresh, stale) * score_scale
        top = jnp.max(scores, axis=1, keepdims=True)
        weights = jnp.exp(scores - top)
        total = jnp.sum(weights, axis=1, keepdims=True)
        probs = weights * (1.0 / total)
        p_fresh[at, :] = jnp.where(fresh_ok, probs, 0.0).astype(jnp.bfloat16)
        p_stale[at, :] = jnp.where(fresh_ok, 0.0, probs).astype(jnp.bfloat16)
        return carry

    lax.fori_loop(0, blocks, probs_block, 0)

    for which in range(3, 5):
        arrived(which)

    per_block = block // slab

    def give_back(i):
        def one(j, carry):
            target = i * per_block + j

            @pl.when(target != me)
            def _():
                pltpu.make_async_remote_copy(
                    src_ref=o_buf.at[row_slab(target, slab), :],
                    dst_ref=out_ref.at[row_slab(my_member, slab), columns(my_head)],
                    send_sem=out_send,
                    recv_sem=out_recv,
                    device_id={"tok": target},
                    device_id_type=MESH,
                ).start()

            return carry

        lax.fori_loop(0, per_block, one, 0)

    def attend_block(i, carry):
        at = row_slab(i, block)
        mixed = jnp.dot(p_fresh[at, :], kv_buf[2], preferred_element_type=jnp.float32)
        mixed = mixed + jnp.dot(p_stale[at, :], kv_buf[3], preferred_element_type=jnp.float32)
        o_buf[at, :] = mixed.astype(jnp.bfloat16)
        give_back(i)
        return carry

    lax.fori_loop(0, blocks, attend_block, 0)
    mine = pltpu.make_async_copy(
        o_buf.at[row_slab(me, slab), :],
        out_ref.at[row_slab(my_member, slab), columns(my_head)],
        own_sem.at[0],
    )
    mine.start()
    for which in range(5):
        view = all_of(which)
        pltpu.make_async_copy(view, view, send_sems.at[which]).wait()
    view = o_buf.at[0 : (devices - 1) * slab, :]
    mine.wait()
    pltpu.make_async_copy(view, view, out_send).wait()
    pltpu.make_async_copy(view, view, out_recv).wait()


def shards(queries, fresh_keys, fresh_values, stale_keys, stale_values, patch_starts, order_starts):
    devices = lax.axis_size("tok")
    tok_dev, width = queries.shape
    slab = tok_dev // (devices // HEADS)
    tokens, rows = devices * tok_dev, devices * slab
    anywhere = pl.BlockSpec(memory_space=pl.ANY)
    scalars = pl.BlockSpec(memory_space=pltpu.SMEM)
    return pl.pallas_call(
        functools.partial(attention_kernel, devices),
        out_shape=jax.ShapeDtypeStruct((tok_dev, width), jnp.bfloat16),
        in_specs=[scalars] * 2 + [anywhere] * 5,
        out_specs=pl.BlockSpec(memory_space=pltpu.VMEM),
        scratch_shapes=[
            pltpu.VMEM((rows, HEAD_DIM), jnp.bfloat16),
            pltpu.VMEM((4, tokens, HEAD_DIM), jnp.bfloat16),
            pltpu.VMEM((rows, tokens), jnp.bfloat16),
            pltpu.VMEM((rows, tokens), jnp.bfloat16),
            pltpu.VMEM((rows, HEAD_DIM), jnp.bfloat16),
            pltpu.VMEM((rows, HEAD_DIM), jnp.int32),
            pltpu.VMEM((8, tokens), jnp.int32),
            pltpu.SemaphoreType.DMA((5,)),
            pltpu.SemaphoreType.DMA((5,)),
            pltpu.SemaphoreType.DMA((5,)),
            pltpu.SemaphoreType.DMA,
            pltpu.SemaphoreType.DMA,
        ],
        compiler_params=pltpu.CompilerParams(
            collective_id=0, has_side_effects=True, vmem_limit_bytes=60 * 1024 * 1024
        ),
    )(
        patch_starts,
        order_starts,
        queries,
        fresh_keys,
        stale_keys,
        fresh_values,
        stale_values,
    )


def solution(mesh):
    placed = (P(("groups", "tok"), None),) * 5 + (P("groups"),) * 2
    return jax.shard_map(
        shards, mesh=mesh, in_specs=placed, out_specs=P(("groups", "tok"), None), check_vma=False
    )
```

time: 72.7 us -> 45.5 us (0.63)
  Pallas kernels: 0 us -> 43 us
  waiting for transfers between devices: 31.5 us -> 0 us
  starting transfers between devices: 14.3 us -> 0 us
  blocking collectives: 12.7 us -> 0 us
  local copies, waits for them, and re-layouts: 7.16 us -> 1.67 us
  matrix products: 4.5 us -> 0 us
  other arithmetic: 1.96 us -> 0 us
    pallas_call x0 -> x1, Pallas kernels: none -> 43 us  [shards(): pl.pallas_call(functools.partial(attention_kernel, devices), out_shape=ja...]
    all_to_all x2 -> x0, waiting for transfers between devices: 31.5 us -> none  [the longest x1 22 us: shards(): lax.all_to_all(spread, 'tok', split_axis=1, concat_axis=1, tiled=True)]
    all_to_all x2 -> x0, starting transfers between devices: 14.3 us -> none  [the longest x1 7.52 us: shards(): lax.all_to_all(spread, 'tok', split_axis=1, concat_axis=1, tiled=True)]
    all_to_all x1 -> x0, blocking collectives: 12.7 us -> none  [shards(): lax.all_to_all(attended.reshape(devices, slab_rows, HEAD_DIM), 'tok', spl...]
    dot_general x8 -> x0, matrix products: 4.5 us -> none  [the longest x2 1.24 us: attend_block(): jnp.dot(stale_probs, key_stack[3], preferred_element_type=jnp.float32)]
    unnamed x12 -> x1, local copies, waits for them, and re-layouts: 4.77 us -> 1.67 us
    reduce_sum x5 -> x0, other arithmetic: 1.72 us -> none  [the longest x2 1.43 us: attend_block(): jnp.sum(stale_exp, axis=1, keepdims=True)]
    transpose x2 -> x0, local copies, waits for them, and re-layouts: 1.44 us -> none  [the longest x1 1.26 us: shards(): by_head = stacked.transpose(0, 2, 1, 3)[:, :, None]]
  transfers between devices with their start and end apart: 2 -> 0, of which waited for: 2 -> 0; matrix products, arithmetic and copies ran while one was open for 2% -> 0% of each run, Pallas kernels for 0% -> 0%
where the time goes in v1:
time: 45.5 us; the launch traced here: 44.7 us
  Pallas kernels  43 us (95%)
  local copies, waits for them, and re-layouts  1.67 us (4%)
    pallas_call x1, Pallas kernels, shards(): pl.pallas_call(functools.partial(attention_kernel, devices), out_shape=ja...  43 us
    unnamed x1, local copies, waits for them, and re-layouts  1.67 us

profile of v1, /device:TPU:0, one launch (start us, length us, event | category | flops | bytes accessed | tf_op | source)
XLA Modules:
  0.0 44.7 jit_solution(12385320494137979462)
XLA Ops:
  0.0 43.0 %shard_map.73 = bf16[64,2048]{1,0:T(8,128)(2,1)} custom-call(s32[16]{0:T(128)} %patch_starts.1, s32[16]{0:T(128)} %order_starts.1, bf16[64,2048]{1,0:T(8,128)(2,1)} %queries.1, bf16[64,2048]{1,0:T(8,128)(2,1)} %fresh_keys.1, bf16[64,2048]{1,0:T(8,128)(2,1)} %stale_keys.1, bf16[64,2048]{1,0:T(8,128)(2,1)} %fresh_values.1, bf16[64,2048]{1,0:T(8,128)(2,1)} %stale_values.1), custom_call_target="tpu_custom_call" | custom-call | tf_op jit(solution)/shard_map/pallas_call | solution.py:218
  43.0 1.7 %copy.9 = bf16[64,2048]{1,0:T(8,128)(2,1)} copy(bf16[64,2048]{1,0:T(8,128)(2,1)} %shard_map.73) | data formatting | bytes 524288

commit v2 on v1

--- a/solution.py
+++ b/solution.py
@@ -219,7 +219,7 @@
         functools.partial(attention_kernel, devices),
         out_shape=jax.ShapeDtypeStruct((tok_dev, width), jnp.bfloat16),
         in_specs=[scalars] * 2 + [anywhere] * 5,
-        out_specs=pl.BlockSpec(memory_space=pltpu.VMEM),
+        out_specs=anywhere,
         scratch_shapes=[
             pltpu.VMEM((rows, HEAD_DIM), jnp.bfloat16),
             pltpu.VMEM((4, tokens, HEAD_DIM), jnp.bfloat16),
@@ -248,8 +248,377 @@
     )
 
 
+def rank_table(patch_starts, order_starts):
+    patches = patch_starts.shape[0]
+    starts = [patch_starts[p] for p in range(patches)]
+    orders = [order_starts[p] for p in range(patches)]
+    ranks = []
+    for p in range(patches):
+        rank = jnp.int32(0)
+        for i in range(patches):
+            rank = rank + jnp.where(orders[i] == starts[p], jnp.int32(i), jnp.int32(0))
+        ranks.append(rank)
+    jumps = [ranks[0]] + [ranks[p] - ranks[p - 1] for p in range(1, patches)]
+
+    def rank_at(positions):
+        total = jnp.zeros(positions.shape, jnp.int32)
+        for p in range(patches):
+            total = total + jnp.where(positions >= starts[p], jumps[p], 0)
+        return total
+
+    return rank_at
+
+
+def halves_kernel(
+    devices,
+    patch_starts,
+    order_starts,
+    queries,
+    fresh_keys,
+    stale_keys,
+    fresh_values,
+    stale_values,
+    parts_ref,
+    stats_ref,
+    q_buf,
+    kv_buf,
+    p_fresh,
+    p_stale,
+    o_buf,
+    s_buf,
+    q_rank,
+    k_rank,
+    q_send,
+    q_recv,
+    kv_send,
+    kv_recv,
+    own_sem,
+    own_kv_sem,
+    o_send,
+    o_recv,
+    s_send,
+    s_recv,
+):
+    me = lax.axis_index("tok")
+    tok_dev = queries.shape[0]
+    half = devices // 2
+    held = HEADS // half
+    tokens = devices * tok_dev
+    keys = half * tok_dev
+    side, place = me // half, me % half
+    barrier = pltpu.get_barrier_semaphore()
+
+    def peer_of(step):
+        return lax.rem(me + step, devices)
+
+    def near_peer(step):
+        return side * half + lax.rem(place + step, half)
+
+    def columns(start, count=1):
+        return pl.ds(pl.multiple_of(start * HEAD_DIM, HEAD_DIM), count * HEAD_DIM)
+
+    def row_slab(index, size):
+        return pl.ds(pl.multiple_of(index * size, size), size)
+
+    def greet(step, carry):
+        pl.semaphore_signal(barrier, inc=1, device_id={"tok": peer_of(step)}, device_id_type=MESH)
+        return carry
+
+    lax.fori_loop(1, devices, greet, 0)
+
+    sources = (fresh_keys, stale_keys, fresh_values, stale_values)
+
+    def q_source(device):
+        return queries.at[:, columns(device % half * held, held)]
+
+    def kv_source(head, which, device):
+        return sources[which].at[:, columns(device % half * held + head)]
+
+    def q_landing(device):
+        return q_buf.at[row_slab(device, tok_dev), :]
+
+    def kv_landing(head, which, device):
+        return kv_buf.at[head, which, row_slab(device % half, tok_dev), :]
+
+    own_q = pltpu.make_async_copy(q_source(me), q_landing(me), own_sem.at[0])
+    own_q.start()
+    own_kv = [
+        [
+            pltpu.make_async_copy(
+                kv_source(head, which, me), kv_landing(head, which, me), own_kv_sem.at[head, which]
+            )
+            for which in range(4)
+        ]
+        for head in range(held)
+    ]
+    for group in own_kv:
+        for copy in group:
+            copy.start()
+    pl.semaphore_wait(barrier, devices - 1)
+
+    def send_q(step, carry):
+        peer = peer_of(step)
+        pltpu.make_async_remote_copy(
+            src_ref=q_source(peer),
+            dst_ref=q_landing(me),
+            send_sem=q_send,
+            recv_sem=q_recv,
+            device_id={"tok": peer},
+            device_id_type=MESH,
+        ).start()
+        return carry
+
+    lax.fori_loop(1, devices, send_q, 0)
+    for head in range(held):
+        for which in range(4):
+
+            def send_kv(step, carry, head=head, which=which):
+                peer = near_peer(step)
+                pltpu.make_async_remote_copy(
+                    src_ref=kv_source(head, which, peer),
+                    dst_ref=kv_landing(head, which, me),
+                    send_sem=kv_send.at[head, which],
+                    recv_sem=kv_recv.at[head, which],
+                    device_id={"tok": peer},
+                    device_id_type=MESH,
+                ).start()
+                return carry
+
+            lax.fori_loop(1, half, send_kv, 0)
+
+    rank_at = rank_table(patch_starts, order_starts)
+    k_rank[...] = rank_at(keys * side + lax.broadcasted_iota(jnp.int32, k_rank.shape, 1))
+
+    def fill_rank(device, carry):
+        q_rank[row_slab(device, tok_dev), :] = rank_at(
+            device * tok_dev + lax.broadcasted_iota(jnp.int32, (tok_dev, HEAD_DIM), 0)
+        )
+        return carry
+
+    lax.fori_loop(0, devices, fill_rank, 0)
+
+    def whole_wait(view, sem):
+        pltpu.make_async_copy(view, view, sem).wait()
+
+    q_all = q_buf.at[0 : (devices - 1) * tok_dev, :]
+
+    def kv_all(head, which):
+        return kv_buf.at[head, which, 0 : (half - 1) * tok_dev, :]
+
+    def arrived(head, which):
+        whole_wait(kv_all(head, which), kv_recv.at[head, which])
+        own_kv[head][which].wait()
+
+    whole_wait(q_all, q_recv)
+    own_q.wait()
+
+    score_scale = 1.0 / math.sqrt(HEAD_DIM)
+    block = min(tokens, 256)
+    blocks = tokens // block
+    per_block = block // tok_dev
+    dims = (((1,), (1,)), ((), ()))
+    first_block = me // per_block + blocks // 2
+    owner_tile = 128 // tok_dev
+
+    for head in range(held):
+        own_columns = slice(head * HEAD_DIM, (head + 1) * HEAD_DIM)
+        arrived(head, 0)
+        arrived(head, 1)
+
+        def probs_block(i, carry, head=head, own_columns=own_columns):
+            at = row_slab(i, block)
+            q = q_buf[at, own_columns]
+            fresh = lax.dot_general(q, kv_buf[head, 0], dims, preferred_element_type=jnp.float32)
+            stale = lax.dot_general(q, kv_buf[head, 1], dims, preferred_element_type=jnp.float32)
+            fresh_ok = k_rank[0:1, :] <= q_rank[at, 0:1]
+            scores = jnp.where(fresh_ok, fresh, stale) * score_scale
+            top = jnp.max(scores, axis=1, keepdims=True)
+            weights = jnp.exp(scores - top)
+            total = jnp.sum(weights, axis=1, keepdims=True)
+            probs = weights * (1.0 / total)
+            p_fresh[at, :] = jnp.where(fresh_ok, probs, 0.0).astype(jnp.bfloat16)
+            p_stale[at, :] = jnp.where(fresh_ok, 0.0, probs).astype(jnp.bfloat16)
+            level = jnp.broadcast_to(top + jnp.log(total), (block, 128))
+            for tile in range(block // 128):
+                turned = jnp.transpose(level[tile * 128 : (tile + 1) * 128, :])
+                s_buf[i * (block // 128) + tile, head : head + 1, :] = turned[0:1, :]
+            return carry
+
+        lax.fori_loop(0, blocks, probs_block, 0)
+        arrived(head, 2)
+        arrived(head, 3)
+
+        if head == held - 1:
+
+            def send_stats(step, carry):
+                peer = peer_of(step)
+                pltpu.make_async_remote_copy(
+                    src_ref=s_buf.at[peer // owner_tile],
+                    dst_ref=stats_ref.at[me],
+                    send_sem=s_send,
+                    recv_sem=s_recv,
+                    device_id={"tok": peer},
+                    device_id_type=MESH,
+                ).start()
+                return carry
+
+        def attend_block(t, carry, head=head):
+            i = lax.rem(first_block + t, blocks)
+            at = row_slab(i, block)
+            mixed = jnp.dot(p_fresh[at, :], kv_buf[head, 2], preferred_element_type=jnp.float32)
+            mixed = mixed + jnp.dot(
+                p_stale[at, :], kv_buf[head, 3], preferred_element_type=jnp.float32
+            )
+            o_buf[head, at, :] = mixed.astype(jnp.bfloat16)
+
+            def give_back(j, carry):
+                target = i * per_block + j
+
+                @pl.when(target != me)
+                def _():
+                    pltpu.make_async_remote_copy(
+                        src_ref=o_buf.at[head, row_slab(target, tok_dev), :],
+                        dst_ref=parts_ref.at[side, :, columns(place * held + head)],
+                        send_sem=o_send.at[head],
+                        recv_sem=o_recv.at[head],
+                        device_id={"tok": target},
+                        device_id_type=MESH,
+                    ).start()
+
+                return carry
+
+            lax.fori_loop(0, per_block, give_back, 0)
+            return carry
+
+        lax.fori_loop(0, blocks, attend_block, 0)
+        if head == held - 1:
+            lax.fori_loop(1, devices, send_stats, 0)
+
+    mine = [
+        pltpu.make_async_copy(
+            o_buf.at[head, row_slab(me, tok_dev), :],
+            parts_ref.at[side, :, columns(place * held + head)],
+            own_sem.at[1 + head],
+        )
+        for head in range(held)
+    ]
+    mine.append(
+        pltpu.make_async_copy(
+            s_buf.at[me // owner_tile], stats_ref.at[me], own_sem.at[1 + held]
+        )
+    )
+    for copy in mine:
+        copy.start()
+    whole_wait(q_all, q_send)
+    for head in range(held):
+        for which in range(4):
+            whole_wait(kv_all(head, which), kv_send.at[head, which])
+    for copy in mine:
+        copy.wait()
+    s_all = stats_ref.at[0 : devices - 1]
+    whole_wait(s_all, s_send)
+    whole_wait(s_all, s_recv)
+    for head in range(held):
+        o_all = o_buf.at[head, 0 : (devices - 1) * tok_dev, :]
+        whole_wait(o_all, o_send.at[head])
+        whole_wait(o_all, o_recv.at[head])
+
+
+def merge_kernel(devices, parts, stats, out_ref, shares):
+    me = lax.axis_index("tok")
+    tok_dev = out_ref.shape[0]
+    half = devices // 2
+    held = HEADS // half
+
+    def levels(side):
+        return jnp.concatenate(
+            [
+                stats[side * half + head // held, head % held : head % held + 1, :]
+                for head in range(HEADS)
+            ],
+            axis=0,
+        )
+
+    low, high = levels(0), levels(1)
+    share = jnp.concatenate(
+        [
+            1.0 / (1.0 + jnp.exp(high - low)),
+            1.0 / (1.0 + jnp.exp(low - high)),
+            jnp.zeros((128 - 2 * HEADS, 128), jnp.float32),
+        ],
+        axis=0,
+    )
+    shares[...] = jnp.transpose(share)
+    start = pl.multiple_of(me % (128 // tok_dev) * tok_dev, tok_dev)
+    mine = shares[pl.ds(start, tok_dev), :]
+    for head in range(HEADS):
+        at = slice(head * HEAD_DIM, (head + 1) * HEAD_DIM)
+        merged = parts[0, :, at].astype(jnp.float32) * mine[:, head : head + 1]
+        merged = merged + parts[1, :, at].astype(jnp.float32) * mine[:, HEADS + head : HEADS + head + 1]
+        out_ref[:, at] = merged.astype(jnp.bfloat16)
+
+
+def halves(queries, fresh_keys, fresh_values, stale_keys, stale_values, patch_starts, order_starts):
+    devices = lax.axis_size("tok")
+    tok_dev, width = queries.shape
+    half = devices // 2
+    held = HEADS // half
+    tokens, keys = devices * tok_dev, half * tok_dev
+    anywhere = pl.BlockSpec(memory_space=pl.ANY)
+    scalars = pl.BlockSpec(memory_space=pltpu.SMEM)
+    vmem = pl.BlockSpec(memory_space=pltpu.VMEM)
+    dma = pltpu.SemaphoreType.DMA
+    parts, stats = pl.pallas_call(
+        functools.partial(halves_kernel, devices),
+        out_shape=(
+            jax.ShapeDtypeStruct((2, tok_dev, width), jnp.bfloat16),
+            jax.ShapeDtypeStruct((devices, held, 128), jnp.float32),
+        ),
+        in_specs=[scalars] * 2 + [anywhere] * 5,
+        out_specs=(anywhere, anywhere),
+        scratch_shapes=[
+            pltpu.VMEM((tokens, held * HEAD_DIM), jnp.bfloat16),
+            pltpu.VMEM((held, 4, keys, HEAD_DIM), jnp.bfloat16),
+            pltpu.VMEM((tokens, keys), jnp.bfloat16),
+            pltpu.VMEM((tokens, keys), jnp.bfloat16),
+            pltpu.VMEM((held, tokens, HEAD_DIM), jnp.bfloat16),
+            pltpu.VMEM((tokens // 128, held, 128), jnp.float32),
+            pltpu.VMEM((tokens, HEAD_DIM), jnp.int32),
+            pltpu.VMEM((8, keys), jnp.int32),
+            dma,
+            dma,
+            dma((held, 4)),
+            dma((held, 4)),
+            dma((2 + held,)),
+            dma((held, 4)),
+            dma((held,)),
+            dma((held,)),
+            dma,
+            dma,
+        ],
+        compiler_params=pltpu.CompilerParams(
+            collective_id=0, has_side_effects=True, vmem_limit_bytes=60 * 1024 * 1024
+        ),
+    )(patch_starts, order_starts, queries, fresh_keys, stale_keys, fresh_values, stale_values)
+    return pl.pallas_call(
+        functools.partial(merge_kernel, devices),
+        out_shape=jax.ShapeDtypeStruct((tok_dev, width), jnp.bfloat16),
+        in_specs=[vmem, vmem],
+        out_specs=vmem,
+        scratch_shapes=[pltpu.VMEM((128, 128), jnp.float32)],
+    )(parts, stats)
+
+
 def solution(mesh):
     placed = (P(("groups", "tok"), None),) * 5 + (P("groups"),) * 2
+    devices = mesh.shape["tok"]
+
+    def body(*arrays):
+        tok_dev = arrays[0].shape[0]
+        split = devices % 2 == 0 and HEADS % (devices // 2) == 0
+        split = split and 128 % tok_dev == 0 and devices * tok_dev % 256 == 0
+        return (halves if split else shards)(*arrays)
+
     return jax.shard_map(
-        shards, mesh=mesh, in_specs=placed, out_specs=P(("groups", "tok"), None), check_vma=False
+        body, mesh=mesh, in_specs=placed, out_specs=P(("groups", "tok"), None), check_vma=False
     )

time: 45.5 us -> 41.2 us (0.905); the launches traced: 44.7 us -> 41.1 us
  Pallas kernels: 43 us -> 41.1 us
  local copies, waits for them, and re-layouts: 1.67 us -> 0 us
    pallas_call x1 -> x2, Pallas kernels: 43 us -> 41.1 us  [the longest x1 38.8 us: halves(): pl.pallas_call(functools.partial(halves_kernel, devices), out_shape=(jax....]
    unnamed x1 -> x0, local copies, waits for them, and re-layouts: 1.67 us -> none
where the time goes in v2:
time: 41.2 us; the launch traced here: 41.1 us
  Pallas kernels  41.1 us (100%)
    pallas_call x1, Pallas kernels, halves(): pl.pallas_call(functools.partial(halves_kernel, devices), out_shape=(jax....  38.8 us
    pallas_call x1, Pallas kernels, halves(): pl.pallas_call(functools.partial(merge_kernel, devices), out_shape=jax.Sh...  2.3 us

profile of v2, /device:TPU:0, one launch (start us, length us, event | category | flops | bytes accessed | tf_op | source)
XLA Modules:
  0.0 41.1 jit_solution(10882233206867713878)
XLA Ops:
  0.0 38.8 %shard_map.73 = (bf16[2,64,2048]{2,1,0:T(8,128)(2,1)}, f32[16,2,128]{2,1,0:T(2,128)}) custom-call(s32[16]{0:T(128)} %patch_starts.1, s32[16]{0:T(128)} %order_starts.1, bf16[64,2048]{1,0:T(8,128)(2,1)} %queries.1, bf16[64,2048]{1,0:T(8,128)(2,1)} %fresh_keys.1, bf16[64,2048]{1,0:T(8,128)(2,1)} %stale_keys.1, bf16[64,2048]{1,0:T(8,128)(2,1)} %fresh_values.1, ...), custom_call_target="tpu_custom_call" | custom-call | tf_op jit(solution)/shard_map/pallas_call | solution.py:571
  38.8 2.3 %shard_map.74 = bf16[64,2048]{1,0:T(8,128)(2,1)} custom-call(bf16[2,64,2048]{2,1,0:T(8,128)(2,1)} %get-tuple-element.7.parts, f32[16,2,128]{2,1,0:T(2,128)} %get-tuple-element.8.stats), custom_call_target="tpu_custom_call" | custom-call | tf_op jit(solution)/shard_map/pallas_call | solution.py:603

commit v3 on v2

--- a/solution.py
+++ b/solution.py
@@ -279,13 +279,15 @@
     fresh_values,
     stale_values,
     parts_ref,
-    stats_ref,
+    shares_ref,
     q_buf,
     kv_buf,
     p_fresh,
     p_stale,
     o_buf,
     s_buf,
+    stats_ref,
+    shares,
     q_rank,
     k_rank,
     q_send,
@@ -490,9 +492,9 @@
             lax.fori_loop(0, per_block, give_back, 0)
             return carry
 
-        lax.fori_loop(0, blocks, attend_block, 0)
         if head == held - 1:
             lax.fori_loop(1, devices, send_stats, 0)
+        lax.fori_loop(0, blocks, attend_block, 0)
 
     mine = [
         pltpu.make_async_copy(
@@ -509,31 +511,14 @@
     )
     for copy in mine:
         copy.start()
-    whole_wait(q_all, q_send)
-    for head in range(held):
-        for which in range(4):
-            whole_wait(kv_all(head, which), kv_send.at[head, which])
-    for copy in mine:
-        copy.wait()
     s_all = stats_ref.at[0 : devices - 1]
-    whole_wait(s_all, s_send)
     whole_wait(s_all, s_recv)
-    for head in range(held):
-        o_all = o_buf.at[head, 0 : (devices - 1) * tok_dev, :]
-        whole_wait(o_all, o_send.at[head])
-        whole_wait(o_all, o_recv.at[head])
-
-
-def merge_kernel(devices, parts, stats, out_ref, shares):
-    me = lax.axis_index("tok")
-    tok_dev = out_ref.shape[0]
-    half = devices // 2
-    held = HEADS // half
-
-    def levels(side):
+    mine[-1].wait()
+
+    def levels(of_side):
         return jnp.concatenate(
             [
-                stats[side * half + head // held, head % held : head % held + 1, :]
+                stats_ref[of_side * half + head // held, head % held : head % held + 1, :]
                 for head in range(HEADS)
             ],
             axis=0,
@@ -549,13 +534,51 @@
         axis=0,
     )
     shares[...] = jnp.transpose(share)
-    start = pl.multiple_of(me % (128 // tok_dev) * tok_dev, tok_dev)
-    mine = shares[pl.ds(start, tok_dev), :]
-    for head in range(HEADS):
-        at = slice(head * HEAD_DIM, (head + 1) * HEAD_DIM)
-        merged = parts[0, :, at].astype(jnp.float32) * mine[:, head : head + 1]
-        merged = merged + parts[1, :, at].astype(jnp.float32) * mine[:, HEADS + head : HEADS + head + 1]
-        out_ref[:, at] = merged.astype(jnp.bfloat16)
+    whole_wait(q_all, q_send)
+    for head in range(held):
+        for which in range(4):
+            whole_wait(kv_all(head, which), kv_send.at[head, which])
+    for copy in mine[:-1]:
+        copy.wait()
+    whole_wait(s_all, s_send)
+    put_shares = pltpu.make_async_copy(
+        shares.at[row_slab(me % owner_tile, tok_dev), :], shares_ref, own_sem.at[0]
+    )
+    put_shares.start()
+    for head in range(held):
+        o_all = o_buf.at[head, 0 : (devices - 1) * tok_dev, :]
+        whole_wait(o_all, o_send.at[head])
+        whole_wait(o_all, o_recv.at[head])
+    put_shares.wait()
+
+
+def merge_kernel(parts_in, shares_in, out_ref, parts, mine, merged, sems, out_sems):
+    width = out_ref.shape[1]
+    chunks = out_sems.shape[0]
+    wide = width // chunks
+    spans = [pl.ds(chunk * wide, wide) for chunk in range(chunks)]
+    shares_copy = pltpu.make_async_copy(shares_in, mine, sems.at[chunks])
+    shares_copy.start()
+    copies = [
+        pltpu.make_async_copy(parts_in.at[:, :, at], parts.at[:, :, at], sems.at[chunk])
+        for chunk, at in enumerate(spans)
+    ]
+    for copy in copies:
+        copy.start()
+    shares_copy.wait()
+    outs = []
+    for chunk, span in enumerate(spans):
+        copies[chunk].wait()
+        for head in range(chunk * wide // HEAD_DIM, (chunk + 1) * wide // HEAD_DIM):
+            at = slice(head * HEAD_DIM, (head + 1) * HEAD_DIM)
+            low = parts[0, :, at].astype(jnp.float32) * mine[:, head : head + 1]
+            high = parts[1, :, at].astype(jnp.float32) * mine[:, HEADS + head : HEADS + head + 1]
+            merged[:, at] = (low + high).astype(jnp.bfloat16)
+        out = pltpu.make_async_copy(merged.at[:, span], out_ref.at[:, span], out_sems.at[chunk])
+        out.start()
+        outs.append(out)
+    for out in outs:
+        out.wait()
 
 
 def halves(queries, fresh_keys, fresh_values, stale_keys, stale_values, patch_starts, order_starts):
@@ -566,13 +589,12 @@
     tokens, keys = devices * tok_dev, half * tok_dev
     anywhere = pl.BlockSpec(memory_space=pl.ANY)
     scalars = pl.BlockSpec(memory_space=pltpu.SMEM)
-    vmem = pl.BlockSpec(memory_space=pltpu.VMEM)
     dma = pltpu.SemaphoreType.DMA
-    parts, stats = pl.pallas_call(
+    parts, shares = pl.pallas_call(
         functools.partial(halves_kernel, devices),
         out_shape=(
             jax.ShapeDtypeStruct((2, tok_dev, width), jnp.bfloat16),
-            jax.ShapeDtypeStruct((devices, held, 128), jnp.float32),
+            jax.ShapeDtypeStruct((tok_dev, 128), jnp.float32),
         ),
         in_specs=[scalars] * 2 + [anywhere] * 5,
         out_specs=(anywhere, anywhere),
@@ -583,6 +605,8 @@
             pltpu.VMEM((tokens, keys), jnp.bfloat16),
             pltpu.VMEM((held, tokens, HEAD_DIM), jnp.bfloat16),
             pltpu.VMEM((tokens // 128, held, 128), jnp.float32),
+            pltpu.VMEM((devices, held, 128), jnp.float32),
+            pltpu.VMEM((128, 128), jnp.float32),
             pltpu.VMEM((tokens, HEAD_DIM), jnp.int32),
             pltpu.VMEM((8, keys), jnp.int32),
             dma,
@@ -601,12 +625,19 @@
         ),
     )(patch_starts, order_starts, queries, fresh_keys, stale_keys, fresh_values, stale_values)
     return pl.pallas_call(
-        functools.partial(merge_kernel, devices),
+        merge_kernel,
         out_shape=jax.ShapeDtypeStruct((tok_dev, width), jnp.bfloat16),
-        in_specs=[vmem, vmem],
-        out_specs=vmem,
-        scratch_shapes=[pltpu.VMEM((128, 128), jnp.float32)],
-    )(parts, stats)
+        in_specs=[anywhere, anywhere],
+        out_specs=anywhere,
+        scratch_shapes=[
+            pltpu.VMEM((2, tok_dev, width), jnp.bfloat16),
+            pltpu.VMEM((tok_dev, 128), jnp.float32),
+            pltpu.VMEM((tok_dev, width), jnp.bfloat16),
+            dma((5,)),
+            dma((4,)),
+        ],
+        compiler_params=pltpu.CompilerParams(vmem_limit_bytes=60 * 1024 * 1024),
+    )(parts, shares)
 
 
 def solution(mesh):

time: 41.2 us -> 40.2 us (0.976)
  Pallas kernels: 41.1 us -> 40 us
    pallas_call x1, Pallas kernels: 38.8 us -> 37.8 us  [halves(): pl.pallas_call(functools.partial(halves_kernel, devices), out_shape=(jax....]
where the time goes in v3:
time: 40.2 us; the launch traced here: 40 us
  Pallas kernels  40 us (100%)
    pallas_call x1, Pallas kernels, halves(): pl.pallas_call(functools.partial(halves_kernel, devices), out_shape=(jax....  37.8 us
    pallas_call x1, Pallas kernels, halves(): pl.pallas_call(merge_kernel, out_shape=jax.ShapeDtypeStruct((tok_dev, wid...  2.23 us

profile of v3, /device:TPU:0, one launch (start us, length us, event | category | flops | bytes accessed | tf_op | source)
XLA Modules:
  0.0 40.0 jit_solution(7253985972542396830)
XLA Ops:
  0.0 37.8 %shard_map.73 = (bf16[2,64,2048]{2,1,0:T(8,128)(2,1)}, f32[64,128]{1,0:T(8,128)}) custom-call(s32[16]{0:T(128)} %patch_starts.1, s32[16]{0:T(128)} %order_starts.1, bf16[64,2048]{1,0:T(8,128)(2,1)} %queries.1, bf16[64,2048]{1,0:T(8,128)(2,1)} %fresh_keys.1, bf16[64,2048]{1,0:T(8,128)(2,1)} %stale_keys.1, bf16[64,2048]{1,0:T(8,128)(2,1)} %fresh_values.1, ...), custom_call_target="tpu_custom_call" | custom-call | tf_op jit(solution)/shard_map/pallas_call | solution.py:593
  37.8 2.2 %shard_map.74 = bf16[64,2048]{1,0:T(8,128)(2,1)} custom-call(bf16[2,64,2048]{2,1,0:T(8,128)(2,1)} %get-tuple-element.7.parts_in, f32[64,128]{1,0:T(8,128)} %get-tuple-element.8.shares_in), custom_call_target="tpu_custom_call" | custom-call | tf_op jit(solution)/shard_map/pallas_call | solution.py:627

commit v4 on v3

--- a/solution.py
+++ b/solution.py
@@ -294,6 +294,7 @@
     q_recv,
     kv_send,
     kv_recv,
+    own_q_sem,
     own_sem,
     own_kv_sem,
     o_send,
@@ -316,8 +317,8 @@
     def near_peer(step):
         return side * half + lax.rem(place + step, half)
 
-    def columns(start, count=1):
-        return pl.ds(pl.multiple_of(start * HEAD_DIM, HEAD_DIM), count * HEAD_DIM)
+    def columns(head):
+        return pl.ds(pl.multiple_of(head * HEAD_DIM, HEAD_DIM), HEAD_DIM)
 
     def row_slab(index, size):
         return pl.ds(pl.multiple_of(index * size, size), size)
@@ -330,20 +331,24 @@
 
     sources = (fresh_keys, stale_keys, fresh_values, stale_values)
 
-    def q_source(device):
-        return queries.at[:, columns(device % half * held, held)]
+    def q_source(head, device):
+        return queries.at[:, columns(device % half * held + head)]
 
     def kv_source(head, which, device):
         return sources[which].at[:, columns(device % half * held + head)]
 
-    def q_landing(device):
-        return q_buf.at[row_slab(device, tok_dev), :]
+    def q_landing(head, device):
+        return q_buf.at[head, row_slab(device, tok_dev), :]
 
     def kv_landing(head, which, device):
         return kv_buf.at[head, which, row_slab(device % half, tok_dev), :]
 
-    own_q = pltpu.make_async_copy(q_source(me), q_landing(me), own_sem.at[0])
-    own_q.start()
+    own_q = [
+        pltpu.make_async_copy(q_source(head, me), q_landing(head, me), own_q_sem.at[head])
+        for head in range(held)
+    ]
+    for copy in own_q:
+        copy.start()
     own_kv = [
         [
             pltpu.make_async_copy(
@@ -358,20 +363,21 @@
             copy.start()
     pl.semaphore_wait(barrier, devices - 1)
 
-    def send_q(step, carry):
-        peer = peer_of(step)
-        pltpu.make_async_remote_copy(
-            src_ref=q_source(peer),
-            dst_ref=q_landing(me),
-            send_sem=q_send,
-            recv_sem=q_recv,
-            device_id={"tok": peer},
-            device_id_type=MESH,
-        ).start()
-        return carry
-
-    lax.fori_loop(1, devices, send_q, 0)
     for head in range(held):
+
+        def send_q(step, carry, head=head):
+            peer = peer_of(step)
+            pltpu.make_async_remote_copy(
+                src_ref=q_source(head, peer),
+                dst_ref=q_landing(head, me),
+                send_sem=q_send.at[head],
+                recv_sem=q_recv.at[head],
+                device_id={"tok": peer},
+                device_id_type=MESH,
+            ).start()
+            return carry
+
+        lax.fori_loop(1, devices, send_q, 0)
         for which in range(4):
 
             def send_kv(step, carry, head=head, which=which):
@@ -402,7 +408,8 @@
     def whole_wait(view, sem):
         pltpu.make_async_copy(view, view, sem).wait()
 
-    q_all = q_buf.at[0 : (devices - 1) * tok_dev, :]
+    def q_all(head):
+        return q_buf.at[head, 0 : (devices - 1) * tok_dev, :]
 
     def kv_all(head, which):
         return kv_buf.at[head, which, 0 : (half - 1) * tok_dev, :]
@@ -411,11 +418,8 @@
         whole_wait(kv_all(head, which), kv_recv.at[head, which])
         own_kv[head][which].wait()
 
-    whole_wait(q_all, q_recv)
-    own_q.wait()
-
     score_scale = 1.0 / math.sqrt(HEAD_DIM)
-    block = min(tokens, 256)
+    block = min(tokens, 512)
     blocks = tokens // block
     per_block = block // tok_dev
     dims = (((1,), (1,)), ((), ()))
@@ -423,13 +427,14 @@
     owner_tile = 128 // tok_dev
 
     for head in range(held):
-        own_columns = slice(head * HEAD_DIM, (head + 1) * HEAD_DIM)
+        whole_wait(q_all(head), q_recv.at[head])
+        own_q[head].wait()
         arrived(head, 0)
         arrived(head, 1)
 
-        def probs_block(i, carry, head=head, own_columns=own_columns):
+        def probs_block(i, carry, head=head):
             at = row_slab(i, block)
-            q = q_buf[at, own_columns]
+            q = q_buf[head, at, :]
             fresh = lax.dot_general(q, kv_buf[head, 0], dims, preferred_element_type=jnp.float32)
             stale = lax.dot_general(q, kv_buf[head, 1], dims, preferred_element_type=jnp.float32)
             fresh_ok = k_rank[0:1, :] <= q_rank[at, 0:1]
@@ -534,8 +539,8 @@
         axis=0,
     )
     shares[...] = jnp.transpose(share)
-    whole_wait(q_all, q_send)
     for head in range(held):
+        whole_wait(q_all(head), q_send.at[head])
         for which in range(4):
             whole_wait(kv_all(head, which), kv_send.at[head, which])
     for copy in mine[:-1]:
@@ -599,7 +604,7 @@
         in_specs=[scalars] * 2 + [anywhere] * 5,
         out_specs=(anywhere, anywhere),
         scratch_shapes=[
-            pltpu.VMEM((tokens, held * HEAD_DIM), jnp.bfloat16),
+            pltpu.VMEM((held, tokens, HEAD_DIM), jnp.bfloat16),
             pltpu.VMEM((held, 4, keys, HEAD_DIM), jnp.bfloat16),
             pltpu.VMEM((tokens, keys), jnp.bfloat16),
             pltpu.VMEM((tokens, keys), jnp.bfloat16),
@@ -609,10 +614,11 @@
             pltpu.VMEM((128, 128), jnp.float32),
             pltpu.VMEM((tokens, HEAD_DIM), jnp.int32),
             pltpu.VMEM((8, keys), jnp.int32),
-            dma,
-            dma,
+            dma((held,)),
+            dma((held,)),
             dma((held, 4)),
             dma((held, 4)),
+            dma((held,)),
             dma((2 + held,)),
             dma((held, 4)),
             dma((held,)),
@@ -647,7 +653,7 @@
     def body(*arrays):
         tok_dev = arrays[0].shape[0]
         split = devices % 2 == 0 and HEADS % (devices // 2) == 0
-        split = split and 128 % tok_dev == 0 and devices * tok_dev % 256 == 0
+        split = split and 128 % tok_dev == 0 and devices * tok_dev % 512 == 0
         return (halves if split else shards)(*arrays)
 
     return jax.shard_map(

time: 40.2 us -> 39.2 us (0.975)
  Pallas kernels: 40 us -> 39 us
    pallas_call x1, Pallas kernels: 37.8 us -> 36.7 us  [halves(): pl.pallas_call(functools.partial(halves_kernel, devices), out_shape=(jax....]
where the time goes in v4:
time: 39.2 us; the launch traced here: 39 us
  Pallas kernels  39 us (99%)
    pallas_call x1, Pallas kernels, halves(): pl.pallas_call(functools.partial(halves_kernel, devices), out_shape=(jax....  36.7 us
    pallas_call x1, Pallas kernels, halves(): pl.pallas_call(merge_kernel, out_shape=jax.ShapeDtypeStruct((tok_dev, wid...  2.23 us

profile of v4, /device:TPU:0, one launch (start us, length us, event | category | flops | bytes accessed | tf_op | source)
XLA Modules:
  0.0 39.0 jit_solution(11614226625946249110)
XLA Ops:
  0.0 36.7 %shard_map.73 = (bf16[2,64,2048]{2,1,0:T(8,128)(2,1)}, f32[64,128]{1,0:T(8,128)}) custom-call(s32[16]{0:T(128)} %patch_starts.1, s32[16]{0:T(128)} %order_starts.1, bf16[64,2048]{1,0:T(8,128)(2,1)} %queries.1, bf16[64,2048]{1,0:T(8,128)(2,1)} %fresh_keys.1, bf16[64,2048]{1,0:T(8,128)(2,1)} %stale_keys.1, bf16[64,2048]{1,0:T(8,128)(2,1)} %fresh_values.1, ...), custom_call_target="tpu_custom_call" | custom-call | tf_op jit(solution)/shard_map/pallas_call | solution.py:598
  36.7 2.2 %shard_map.74 = bf16[64,2048]{1,0:T(8,128)(2,1)} custom-call(bf16[2,64,2048]{2,1,0:T(8,128)(2,1)} %get-tuple-element.7.parts_in, f32[64,128]{1,0:T(8,128)} %get-tuple-element.8.shares_in), custom_call_target="tpu_custom_call" | custom-call | tf_op jit(solution)/shard_map/pallas_call | solution.py:633

commit v5 on v4

--- a/solution.py
+++ b/solution.py
@@ -423,7 +423,6 @@
     blocks = tokens // block
     per_block = block // tok_dev
     dims = (((1,), (1,)), ((), ()))
-    first_block = me // per_block + blocks // 2
     owner_tile = 128 // tok_dev
 
     for head in range(held):
@@ -469,8 +468,7 @@
                 ).start()
                 return carry
 
-        def attend_block(t, carry, head=head):
-            i = lax.rem(first_block + t, blocks)
+        def attend_block(i, carry, head=head):
             at = row_slab(i, block)
             mixed = jnp.dot(p_fresh[at, :], kv_buf[head, 2], preferred_element_type=jnp.float32)
             mixed = mixed + jnp.dot(
@@ -639,8 +637,8 @@
             pltpu.VMEM((2, tok_dev, width), jnp.bfloat16),
             pltpu.VMEM((tok_dev, 128), jnp.float32),
             pltpu.VMEM((tok_dev, width), jnp.bfloat16),
-            dma((5,)),
-            dma((4,)),
+            dma((3,)),
+            dma((2,)),
         ],
         compiler_params=pltpu.CompilerParams(vmem_limit_bytes=60 * 1024 * 1024),
     )(parts, shares)

time: 39.2 us -> 39.1 us (level)
  no operation moved by 1% of the time
where the time goes in v5:
time: 39.1 us; the launch traced here: 38.9 us
  Pallas kernels  38.9 us (99%)
    pallas_call x1, Pallas kernels, halves(): pl.pallas_call(functools.partial(halves_kernel, devices), out_shape=(jax....  36.7 us
    pallas_call x1, Pallas kernels, halves(): pl.pallas_call(merge_kernel, out_shape=jax.ShapeDtypeStruct((tok_dev, wid...  2.12 us

profile of v5, /device:TPU:0, one launch (start us, length us, event | category | flops | bytes accessed | tf_op | source)
XLA Modules:
  0.0 38.9 jit_solution(4489406516225208194)
XLA Ops:
  0.0 36.7 %shard_map.73 = (bf16[2,64,2048]{2,1,0:T(8,128)(2,1)}, f32[64,128]{1,0:T(8,128)}) custom-call(s32[16]{0:T(128)} %patch_starts.1, s32[16]{0:T(128)} %order_starts.1, bf16[64,2048]{1,0:T(8,128)(2,1)} %queries.1, bf16[64,2048]{1,0:T(8,128)(2,1)} %fresh_keys.1, bf16[64,2048]{1,0:T(8,128)(2,1)} %stale_keys.1, bf16[64,2048]{1,0:T(8,128)(2,1)} %fresh_values.1, ...), custom_call_target="tpu_custom_call" | custom-call | tf_op jit(solution)/shard_map/pallas_call | solution.py:596
  36.7 2.1 %shard_map.74 = bf16[64,2048]{1,0:T(8,128)(2,1)} custom-call(bf16[2,64,2048]{2,1,0:T(8,128)(2,1)} %get-tuple-element.7.parts_in, f32[64,128]{1,0:T(8,128)} %get-tuple-element.8.shares_in), custom_call_target="tpu_custom_call" | custom-call | tf_op jit(solution)/shard_map/pallas_call | solution.py:631
